TPU v7x, 256 devices: a whole 4x4x8 slice. The times are simulated.
256 devices in a mesh: ctx: 16 (over y, x), head: 4 (over z_lo, core), clip: 4 (over z_hi).
Axes of the slice: x: 4, y: 4, z: 8 (z_hi: 4, z_lo: 2; z = z_hi * 2 + z_lo), core: 2. Of those that a mesh axis runs over, the one named last changes fastest.
Arguments:
- queries: bfloat16 [4, 2048, 2560], P('clip', 'ctx', 'head'), may hold values from -40 to 40
- key_states: bfloat16 [4, 2048, 2560], P('clip', 'ctx', 'head'), may hold values from -40 to 40
- value_states: bfloat16 [4, 2048, 2560], P('clip', 'ctx', 'head'), may hold values from -40 to 40
- layer_grad: bfloat16 [4, 2048, 5120], P('clip', 'ctx'), may hold values from -6 to 6
- out_weight: bfloat16 [2560, 5120], P('head', 'clip'), may hold values from -0.125 to 0.125
- chosen: int32 [4, 32, 4], P('clip', 'ctx'), may hold values from 0 to 31, all different within a row
Outputs:
- attention: bfloat16 [4, 2048, 2560], P('clip', 'ctx', 'head')
- query_grad: bfloat16 [4, 2048, 2560], P('clip', 'ctx', 'head')
- key_grad: bfloat16 [4, 2048, 2560], P('clip', 'ctx', 'head')
- value_grad: bfloat16 [4, 2048, 2560], P('clip', 'ctx', 'head')
- weight_grad: bfloat16 [2560, 5120], P('head', 'clip')
Inputs may be any that keep to these rules, and one draw needn't show every extreme that they name: Each row names 4 different cubes of its clip; how often a key cube is chosen differs widely from cube to cube.
All inputs are finite; a program needn't handle non-finite values.
Results may differ from a plain program's by a relative error of at most 0.025.
Values may be sent and summed in bfloat16 or wider, within the bound.
No kernel may reach another device: no remote copies, remote signals or barrier semaphores. Data moves between devices by JAX's collectives and lax.ppermute only.
A program may use at most 128 MiB of HBM per device.

v0:
```python
import jax
import jax.numpy as jnp
from jax import lax
from jax.sharding import PartitionSpec as P

HD = 128
CUBE = 64


def cube_means(blocks):
    grouped = blocks.astype(jnp.float32).reshape(-1, CUBE, blocks.shape[-1])
    return jnp.mean(grouped, axis=1).astype(jnp.bfloat16)


def by_heads(blocks):
    return blocks.reshape(blocks.shape[0], -1, HD)


def softmax_rows(scores):
    largest = jnp.max(scores, axis=-1, keepdims=True)
    expons = jnp.exp(scores - largest)
    return expons / jnp.sum(expons, axis=-1, keepdims=True)


def on_device(queries, key_states, value_states, layer_grad, out_weight, chosen):
    scaling = HD ** (-0.5)
    query_local = queries[0]
    key_local = key_states[0]
    value_local = value_states[0]
    layer_local = layer_grad[0]
    picked = chosen[0]
    tok_local, width = query_local.shape
    heads_here = width // HD
    cubes_local = tok_local // CUBE
    picks_each = picked.shape[1]
    key_whole, value_whole = (
        lax.all_gather(key_local, "ctx", axis=0, tiled=True),
        lax.all_gather(value_local, "ctx", axis=0, tiled=True),
    )
    tok_whole = key_whole.shape[0]
    cubes_whole = tok_whole // CUBE
    query_cube = cube_means(query_local)
    key_cube, value_cube = (
        lax.all_gather(cube_means(key_local), "ctx", axis=0, tiled=True),
        lax.all_gather(cube_means(value_local), "ctx", axis=0, tiled=True),
    )
    qcube_heads = by_heads(query_cube)
    kcube_heads = by_heads(key_cube)
    vcube_heads = by_heads(value_cube)
    coarse_scores = (
        jnp.einsum("ahd,bhd->hab", qcube_heads, kcube_heads, preferred_element_type=jnp.float32)
        * scaling
    )
    coarse_p = softmax_rows(coarse_scores)
    coarse_half = coarse_p.astype(jnp.bfloat16)
    coarse_out = jnp.einsum(
        "hab,bhd->ahd", coarse_half, vcube_heads, preferred_element_type=jnp.float32
    )
    key_cubes = key_whole.reshape(cubes_whole, CUBE, width)
    value_cubes = value_whole.reshape(cubes_whole, CUBE, width)
    key_pick = key_cubes[picked].reshape(cubes_local, picks_each * CUBE, heads_here, HD)
    value_pick = value_cubes[picked].reshape(cubes_local, picks_each * CUBE, heads_here, HD)
    query_blocks = query_local.reshape(cubes_local, CUBE, heads_here, HD)
    fine_scores = (
        jnp.einsum("cthd,ckhd->chtk", query_blocks, key_pick, preferred_element_type=jnp.float32)
        * scaling
    )
    fine_p = softmax_rows(fine_scores)
    fine_half = fine_p.astype(jnp.bfloat16)
    fine_out = jnp.einsum(
        "chtk,ckhd->cthd", fine_half, value_pick, preferred_element_type=jnp.float32
    )
    attention = (
        (fine_out + coarse_out[:, None, :, :]).astype(jnp.bfloat16).reshape(tok_local, width)
    )
    attn_grad = lax.dot_general(
        layer_local,
        lax.all_gather(out_weight, "clip", axis=1, tiled=True),
        (((1,), (1,)), ((), ())),
        preferred_element_type=jnp.float32,
    ).astype(jnp.bfloat16)
    grad_cube = jnp.sum(
        attn_grad.astype(jnp.float32).reshape(cubes_local, CUBE, width), axis=1
    ).astype(jnp.bfloat16)
    gcube_heads = by_heads(grad_cube)
    coarse_dp = jnp.einsum(
        "ahd,bhd->hab", gcube_heads, vcube_heads, preferred_element_type=jnp.float32
    )
    coarse_delta = jnp.sum(coarse_p * coarse_dp, axis=-1, keepdims=True)
    coarse_ds = (scaling * coarse_p * (coarse_dp - coarse_delta)).astype(jnp.bfloat16)
    coarse_dq = jnp.einsum(
        "hab,bhd->ahd", coarse_ds, kcube_heads, preferred_element_type=jnp.float32
    )
    coarse_dk = jnp.einsum(
        "hab,ahd->bhd", coarse_ds, qcube_heads, preferred_element_type=jnp.float32
    )
    coarse_dv = jnp.einsum(
        "hab,ahd->bhd", coarse_half, gcube_heads, preferred_element_type=jnp.float32
    )
    cube_terms = (
        jnp.concatenate(
            [coarse_dk.reshape(cubes_whole, width), coarse_dv.reshape(cubes_whole, width)], axis=1
        )
        / CUBE
    )
    grad_blocks = attn_grad.reshape(cubes_local, CUBE, heads_here, HD)
    fine_dp = jnp.einsum(
        "cthd,ckhd->chtk", grad_blocks, value_pick, preferred_element_type=jnp.float32
    )
    fine_delta = jnp.sum(fine_p * fine_dp, axis=-1, keepdims=True)
    fine_ds = (scaling * fine_p * (fine_dp - fine_delta)).astype(jnp.bfloat16)
    query_grad = jnp.einsum(
        "chtk,ckhd->cthd", fine_ds, key_pick, preferred_element_type=jnp.float32
    )
    query_grad = (query_grad + coarse_dq[:, None, :, :] / CUBE).astype(jnp.bfloat16)
    query_grad = query_grad.reshape(tok_local, width)
    key_picked = jnp.einsum(
        "chtk,cthd->ckhd", fine_ds, query_blocks, preferred_element_type=jnp.float32
    )
    value_picked = jnp.einsum(
        "chtk,cthd->ckhd", fine_half, grad_blocks, preferred_element_type=jnp.float32
    )
    flat_terms = jnp.concatenate(
        [
            key_picked.reshape(cubes_local, picks_each, CUBE, width),
            value_picked.reshape(cubes_local, picks_each, CUBE, width),
        ],
        axis=3,
    )
    flat_terms = flat_terms.reshape(cubes_local * picks_each, CUBE, 2 * width)
    picked_flat = picked.reshape(-1)
    running = jnp.broadcast_to(cube_terms[:, None, :], (cubes_whole, CUBE, 2 * width))
    running = running.at[picked_flat].add(flat_terms)
    summed = lax.psum_scatter(
        running.reshape(tok_whole, 2 * width).astype(jnp.bfloat16),
        "ctx",
        scatter_dimension=0,
        tiled=True,
    ).astype(jnp.float32)
    key_grad = summed[:, :width].astype(jnp.bfloat16)
    value_grad = summed[:, width:].astype(jnp.bfloat16)
    weight_term = lax.dot_general(
        attention, layer_local, (((0,), (0,)), ((), ())), preferred_element_type=jnp.float32
    )
    over_clips = lax.psum_scatter(
        weight_term.astype(jnp.bfloat16), "clip", scatter_dimension=1, tiled=True
    )
    over_groups = lax.psum(over_clips, "ctx").astype(jnp.float32)
    weight_grad = over_groups.astype(jnp.bfloat16)
    return (attention[None], query_grad[None], key_grad[None], value_grad[None], weight_grad)


def solution(mesh):
    placed = (
        P("clip", "ctx", "head"),
        P("clip", "ctx", "head"),
        P("clip", "ctx", "head"),
        P("clip", "ctx", None),
        P("head", "clip"),
        P("clip", "ctx", None),
    )
    return jax.shard_map(
        on_device,
        mesh=mesh,
        in_specs=placed,
        out_specs=(
            P("clip", "ctx", "head"),
            P("clip", "ctx", "head"),
            P("clip", "ctx", "head"),
            P("clip", "ctx", "head"),
            P("head", "clip"),
        ),
        check_vma=False,
    )
```

profile of v0, /device:TPU:2, one launch (start us, length us, event | category | flops | bytes accessed | tf_op | source)
XLA Modules:
  0.0 575.4 jit_solution(13618390725349178365)
XLA Ops:
  10.2 1.0 convert_reduce_fusion.2
  11.2 23.5 %all-gather.2 = bf16[16,2,640]{2,1,0:T(2,128)(2,1)S(1)} all-gather(bf16[1,2,640]{2,1,0:T(2,128)(2,1)S(1)} %fusion.36), channel_id=1, replica_groups=mesh['ctx'=16,'head'=4,'clip'=4] {'ctx'}, dimensions={0}, use_global_device_ids=true | all-gather | bytes 43520 | tf_op jit(solution)/shard_map/all_gather | solution.py:45
  34.7 1.0 convert_reduce_fusion
  35.7 21.4 %all-gather.3 = bf16[16,2,640]{2,1,0:T(2,128)(2,1)S(1)} all-gather(bf16[1,2,640]{2,1,0:T(2,128)(2,1)S(1)} %fusion.38), channel_id=1, replica_groups=mesh['ctx'=16,'head'=4,'clip'=4] {'ctx'}, dimensions={0}, use_global_device_ids=true | all-gather | bytes 43520 | tf_op jit(solution)/shard_map/all_gather | solution.py:44
  57.7 6.8 %all-gather.10.cloned.1.call-done = bf16[1,2048,640]{2,1,0:T(8,128)(2,1)} async-done(((bf16[1,128,640]{2,1,0:T(8,128)(2,1)}), bf16[1,2048,640]{2,1,0:T(8,128)(2,1)}) %all-gather.10.cloned.1.call-update) | async-done | bytes 2621456 | tf_op jit(solution)/shard_map/all_gather | solution.py:38
  64.5 2.4 gather_fusion
  66.9 1.7 reshape.154
  68.6 49.0 %all-gather.12.cloned.1.call-done = bf16[1,2048,640]{2,1,0:T(8,128)(2,1)} async-done(((bf16[1,128,640]{2,1,0:T(8,128)(2,1)}), bf16[1,2048,640]{2,1,0:T(8,128)(2,1)}) %all-gather.12.cloned.1.call-update) | async-done | bytes 2621456 | tf_op jit(solution)/shard_map/all_gather | solution.py:37
  117.6 2.4 gather_fusion.1
  121.1 1.0 fusion.47
  122.1 111.0 %all-gather.8.cloned.1.call-done = bf16[640,5120]{1,0:T(8,128)(2,1)} async-done(((bf16[640,1280]{1,0:T(8,128)(2,1)}), bf16[640,5120]{1,0:T(8,128)(2,1)}) %all-gather.8.cloned.1.call-update) | async-done | bytes 6553616 | tf_op jit(solution)/shard_map/all_gather | solution.py:78
  233.1 5.0 bitcast_reduce_fusion
  238.5 2.4 fusion.14
  241.8 4.6 convolution_convert_fusion
  248.1 2.4 convolution_bitcast_fusion
  250.5 2.0 copy.84
  252.4 1.4 concatenate.23
  253.8 2.0 multiply_reduce_fusion
  256.1 0.8 copy-done.8
  257.3 0.8 copy.82
  258.1 1.4 concatenate.22
  260.0 3.4 pad_maximum_fusion
  263.5 5.4 broadcast_in_dim.6
  268.9 5.7 scatter_fusion
  274.6 7.0 %convert_element_type.116 = bf16[32,64,1280]{2,1,0:T(8,128)(2,1)} convert(f32[32,64,1280]{2,1,0:T(8,128)} %scatter_fusion) | non-fusion elementwise | flops 2621440 | bytes 15728640 | tf_op jit(solution)/shard_map/convert_element_type | solution.py:135
  281.7 97.3 %reduce-scatter.5.cloned.1.call-done = bf16[640,1280]{1,0:T(8,128)(2,1)} async-done(((bf16[640,5120]{1,0:T(8,128)(2,1)}), bf16[640,1280]{1,0:T(8,128)(2,1)}) %reduce-scatter.5.cloned.1.call-update) | async-done | bytes 1638416 | tf_op jit(solution)/shard_map/reduce_scatter | solution.py:145
  379.1 0.9 broadcast_in_dim_reshape.6
  380.5 0.9 broadcast_in_dim_reshape.7
  381.3 83.5 %reduce-scatter.3.cloned.1.call-done = bf16[128,1280]{1,0:T(8,128)(2,1)} async-done(((bf16[2048,1280]{1,0:T(8,128)(2,1)}), bf16[128,1280]{1,0:T(8,128)(2,1)}) %reduce-scatter.3.cloned.1.call-update) | async-done | bytes 327696 | tf_op jit(solution)/shard_map/reduce_scatter | solution.py:134
  464.8 1.7 slice_bitcast_fusion
  466.6 99.3 %all-reduce.2.cloned.1.call-done = bf16[640,1280]{1,0:T(8,128)(2,1)} async-done(((bf16[640,1280]{1,0:T(8,128)(2,1)}), bf16[640,1280]{1,0:T(8,128)(2,1)}) %all-reduce.2.cloned.1.call-update) | async-done | bytes 1638416 | tf_op jit(solution)/shard_map/psum | solution.py:148
  565.9 2.7 copy.129
  (67 shorter events, 9.3 us)
Async XLA Ops:
  7.2 226.0 %copy-start = (bf16[1,128,5120]{2,1,0:T(8,128)(2,1)S(1)}, bf16[1,128,5120]{2,1,0:T(8,128)(2,1)}, u32[]{:S(2)}) copy-start(bf16[1,128,5120]{2,1,0:T(8,128)(2,1)} %param.9) | copy-start | bytes 3932164
  7.2 49.9 %copy-start.10 = (bf16[1,128,640]{2,1,0:T(8,128)(2,1)S(1)}, bf16[1,128,640]{2,1,0:T(8,128)(2,1)}, u32[]{:S(2)}) copy-start(bf16[1,128,640]{2,1,0:T(8,128)(2,1)} %param.6) | copy-start | bytes 491524
  7.2 57.3 %all-gather.10.cloned.1.call-start = ((), (), s32[]{:S(2)}) async-start(), calls=%async_computation.6 | async-start | bytes 2785280 | tf_op jit(solution)/shard_map/all_gather | solution.py:38
  7.9 109.6 %all-gather.12.cloned.1.call-start = ((), (), s32[]{:S(2)}) async-start(), calls=%async_computation.7 | async-start | bytes 2785280 | tf_op jit(solution)/shard_map/all_gather | solution.py:37
  8.7 224.5 %all-gather.8.cloned.1.call-start = ((), (), s32[]{:S(2)}) async-start(), calls=%async_computation.2 | async-start | bytes 8192000 | tf_op jit(solution)/shard_map/all_gather | solution.py:78
  9.4 369.6 %reduce-scatter.5.cloned.1.call-start = ((), (), s32[]{:S(2)}) async-start(), calls=%async_computation.4 | async-start | bytes 8192000 | tf_op jit(solution)/shard_map/reduce_scatter | solution.py:145
  57.3 63.4 %copy-start.6 = (bf16[2,64,5,128]{3,2,1,0:T(8,128)(2,1)}, bf16[2,64,5,128]{3,2,1,0:T(8,128)(2,1)S(1)}, u32[]{:S(2)}) copy-start(bf16[2,64,5,128]{3,2,1,0:T(8,128)(2,1)S(1)} %reshape_squeeze.6) | copy-start | bytes 491524
  120.7 117.4 %copy-start.1 = (bf16[2,256,5,128]{3,2,1,0:T(8,128)(2,1)}, bf16[2,256,5,128]{3,2,1,0:T(8,128)(2,1)S(1)}, u32[]{:S(2)}) copy-start(bf16[2,256,5,128]{3,2,1,0:T(8,128)(2,1)S(1)} %reshape.156) | copy-start | bytes 1966084
  241.1 0.7 copy-start.4
  246.4 0.7 copy-start.12
  246.4 218.5 %reduce-scatter.3.cloned.1.call-start = ((), (), s32[]{:S(2)}) async-start(), calls=%async_computation.3 | async-start | bytes 5570560 | tf_op jit(solution)/shard_map/reduce_scatter | solution.py:134
  247.3 0.7 copy-start.11
  253.8 2.0 copy-start.3
  253.8 3.0 copy-start.7
  256.1 0.8 copy-start.8
  281.6 97.4 %copy-start.5 = (bf16[2,64,5,128]{3,2,1,0:T(8,128)(2,1)S(1)}, bf16[2,64,5,128]{3,2,1,0:T(8,128)(2,1)}, u32[]{:S(2)}) copy-start(bf16[2,64,5,128]{3,2,1,0:T(8,128)(2,1)} %copy-done.4) | copy-start | bytes 491524
  281.6 98.5 %copy-start.2 = (bf16[2,256,5,128]{3,2,1,0:T(8,128)(2,1)S(1)}, bf16[2,256,5,128]{3,2,1,0:T(8,128)(2,1)}, u32[]{:S(2)}) copy-start(bf16[2,256,5,128]{3,2,1,0:T(8,128)(2,1)} %copy-done.1) | copy-start | bytes 1966084
  281.6 98.5 %copy-start.9 = (bf16[2,5,64,256]{3,2,1,0:T(8,128)(2,1)S(1)}, bf16[2,5,64,256]{3,2,1,0:T(8,128)(2,1)}, u32[]{:S(2)}) copy-start(bf16[2,5,64,256]{3,2,1,0:T(8,128)(2,1)} %copy-done.8) | copy-start | bytes 983044
  281.7 284.2 %all-reduce.2.cloned.1.call-start = ((), (), s32[]{:S(2)}) async-start(), calls=%async_computation.5 | async-start | bytes 3276800 | tf_op jit(solution)/shard_map/psum | solution.py:148
Sparse Core Ops, SparseCore 0:
  10.5 53.9 all-gather.9
  66.9 50.6 all-gather.11
  119.4 113.7 all-gather.7
  246.5 132.4 reduce-scatter.4
  382.5 82.2 reduce-scatter.2
  468.1 97.7 all-reduce.1
where the time goes:
time: 576 us; the launch traced here: 575 us
  waiting for transfers between devices  449 us (78%)
  blocking collectives  44.9 us (8%)
  local copies, waits for them, and re-layouts  28 us (5%)
  other arithmetic  20.2 us (4%)
  matrix products  18.5 us (3%)
  between operations  14.4 us (2%)
    all_gather x1, waiting for transfers between devices, on_device(): lax.all_gather(out_weight, 'clip', axis=1, tiled=True)  111 us
    psum x1, waiting for transfers between devices, on_device(): over_groups = lax.psum(over_clips, 'ctx').astype(jnp.float32)  99.3 us
    reduce_scatter x1, waiting for transfers between devices, on_device(): lax.psum_scatter(weight_term.astype(jnp.bfloat16), 'clip', scatter_dimens...  97.3 us
    reduce_scatter x1, waiting for transfers between devices, on_device(): lax.psum_scatter(running.reshape(tok_whole, 2 * width).astype(jnp.bfloat1...  83.5 us
    all_gather x1, waiting for transfers between devices, on_device(): lax.all_gather(key_local, 'ctx', axis=0, tiled=True)  49 us
    all_gather x1, blocking collectives, on_device(): lax.all_gather(cube_means(value_local), 'ctx', axis=0, tiled=True)  23.5 us
    all_gather x1, blocking collectives, on_device(): lax.all_gather(cube_means(key_local), 'ctx', axis=0, tiled=True)  21.4 us
  transfers between devices with their start and end apart: 6, of which 6 were waited for; matrix products, arithmetic and copies ran while one was open for 8% of the time, Pallas kernels for 0%

commit v1 on v0

--- a/solution.py
+++ b/solution.py
@@ -145,7 +145,7 @@
     over_clips = lax.psum_scatter(
         weight_term.astype(jnp.bfloat16), "clip", scatter_dimension=1, tiled=True
     )
-    over_groups = lax.psum(over_clips, "ctx").astype(jnp.float32)
+    over_groups = jnp.sum(lax.all_gather(over_clips, "ctx"), axis=0).astype(jnp.float32)
     weight_grad = over_groups.astype(jnp.bfloat16)
     return (attention[None], query_grad[None], key_grad[None], value_grad[None], weight_grad)
 

time: 576 us -> 656 us (1.14)
  waiting for transfers between devices: 449 us -> 518 us
  other arithmetic: 20.2 us -> 37 us
    all_gather x0 -> x1, waiting for transfers between devices: none -> 165 us  [on_device(): lax.all_gather(over_clips, 'ctx')]
    psum x1 -> x0, waiting for transfers between devices: 99.3 us -> none  [on_device(): over_groups = lax.psum(over_clips, 'ctx').astype(jnp.float32)]
    reduce_sum x0 -> x1, other arithmetic: none -> 16.8 us  [on_device(): jnp.sum(lax.all_gather(over_clips, 'ctx'), axis=0).astype(jnp.float32)]
  transfers between devices with their start and end apart: 6 -> 6, of which waited for: 6 -> 6; matrix products, arithmetic and copies ran while one was open for 8% -> 7% of each run, Pallas kernels for 0% -> 0%
where the time goes in v1:
time: 656 us; the launch traced here: 655 us
  waiting for transfers between devices  518 us (79%)
  blocking collectives  44.9 us (7%)
  other arithmetic  37 us (6%)
  local copies, waits for them, and re-layouts  22.6 us (3%)
  matrix products  17.5 us (3%)
  between operations  14.4 us (2%)
    all_gather x1, waiting for transfers between devices, on_device(): lax.all_gather(over_clips, 'ctx')  165 us
    all_gather x1, waiting for transfers between devices, on_device(): lax.all_gather(out_weight, 'clip', axis=1, tiled=True)  111 us
    reduce_scatter x1, waiting for transfers between devices, on_device(): lax.psum_scatter(weight_term.astype(jnp.bfloat16), 'clip', scatter_dimens...  101 us
    reduce_scatter x1, waiting for transfers between devices, on_device(): lax.psum_scatter(running.reshape(tok_whole, 2 * width).astype(jnp.bfloat1...  83.3 us
    all_gather x1, waiting for transfers between devices, on_device(): lax.all_gather(key_local, 'ctx', axis=0, tiled=True)  49 us
    all_gather x1, blocking collectives, on_device(): lax.all_gather(cube_means(value_local), 'ctx', axis=0, tiled=True)  23.5 us
    all_gather x1, blocking collectives, on_device(): lax.all_gather(cube_means(key_local), 'ctx', axis=0, tiled=True)  21.4 us
    reduce_sum x1, other arithmetic, on_device(): jnp.sum(lax.all_gather(over_clips, 'ctx'), axis=0).astype(jnp.float32)  16.8 us
  transfers between devices with their start and end apart: 6, of which 6 were waited for; matrix products, arithmetic and copies ran while one was open for 7% of the time, Pallas kernels for 0%

profile of v1, /device:TPU:2, one launch (start us, length us, event | category | flops | bytes accessed | tf_op | source)
XLA Modules:
  0.0 654.8 jit_solution(6809979915041533690)
XLA Ops:
  10.2 1.0 convert_reduce_fusion.2
  11.2 23.5 %all-gather.3 = bf16[16,2,640]{2,1,0:T(2,128)(2,1)S(1)} all-gather(bf16[1,2,640]{2,1,0:T(2,128)(2,1)S(1)} %fusion.36), channel_id=1, replica_groups=mesh['ctx'=16,'head'=4,'clip'=4] {'ctx'}, dimensions={0}, use_global_device_ids=true | all-gather | bytes 43520 | tf_op jit(solution)/shard_map/all_gather | solution.py:45
  34.7 1.0 convert_reduce_fusion
  35.7 21.4 %all-gather.4 = bf16[16,2,640]{2,1,0:T(2,128)(2,1)S(1)} all-gather(bf16[1,2,640]{2,1,0:T(2,128)(2,1)S(1)} %fusion.38), channel_id=1, replica_groups=mesh['ctx'=16,'head'=4,'clip'=4] {'ctx'}, dimensions={0}, use_global_device_ids=true | all-gather | bytes 43520 | tf_op jit(solution)/shard_map/all_gather | solution.py:44
  57.7 6.8 %all-gather.12.cloned.1.call-done = bf16[1,2048,640]{2,1,0:T(8,128)(2,1)} async-done(((bf16[1,128,640]{2,1,0:T(8,128)(2,1)}), bf16[1,2048,640]{2,1,0:T(8,128)(2,1)}) %all-gather.12.cloned.1.call-update) | async-done | bytes 2621456 | tf_op jit(solution)/shard_map/all_gather | solution.py:38
  64.5 2.4 gather_fusion
  66.9 1.7 reshape.154
  68.6 49.0 %all-gather.14.cloned.1.call-done = bf16[1,2048,640]{2,1,0:T(8,128)(2,1)} async-done(((bf16[1,128,640]{2,1,0:T(8,128)(2,1)}), bf16[1,2048,640]{2,1,0:T(8,128)(2,1)}) %all-gather.14.cloned.1.call-update) | async-done | bytes 2621456 | tf_op jit(solution)/shard_map/all_gather | solution.py:37
  117.6 2.4 gather_fusion.1
  120.0 0.7 reshape.156
  121.1 1.0 fusion.47
  122.1 111.0 %all-gather.10.cloned.1.call-done = bf16[640,5120]{1,0:T(8,128)(2,1)} async-done(((bf16[640,1280]{1,0:T(8,128)(2,1)}), bf16[640,5120]{1,0:T(8,128)(2,1)}) %all-gather.10.cloned.1.call-update) | async-done | bytes 6553616 | tf_op jit(solution)/shard_map/all_gather | solution.py:78
  233.1 5.0 bitcast_reduce_fusion
  238.5 2.4 fusion.14
  241.8 4.6 convolution_convert_fusion
  248.0 1.3 convolution_bitcast_fusion
  249.4 1.0 copy.84
  250.8 2.0 multiply_reduce_fusion
  253.0 0.7 copy-done.9
  254.1 0.8 copy.82
  254.9 1.4 concatenate.22
  256.9 3.0 pad_maximum_fusion
  259.9 4.8 broadcast_in_dim.6
  264.7 6.0 scatter_fusion
  270.7 7.1 %convert_element_type.118 = bf16[32,64,1280]{2,1,0:T(8,128)(2,1)} convert(f32[32,64,1280]{2,1,0:T(8,128)} %scatter_fusion) | non-fusion elementwise | flops 2621440 | bytes 15728640 | tf_op jit(solution)/shard_map/convert_element_type | solution.py:135
  277.9 101.1 %reduce-scatter.5.cloned.1.call-done = bf16[640,1280]{1,0:T(8,128)(2,1)} async-done(((bf16[640,5120]{1,0:T(8,128)(2,1)}), bf16[640,1280]{1,0:T(8,128)(2,1)}) %reduce-scatter.5.cloned.1.call-update) | async-done | bytes 1638416 | tf_op jit(solution)/shard_map/reduce_scatter | solution.py:145
  379.1 0.9 broadcast_in_dim_reshape.6
  380.4 0.9 broadcast_in_dim_reshape.7
  381.3 83.3 %reduce-scatter.3.cloned.1.call-done = bf16[128,1280]{1,0:T(8,128)(2,1)} async-done(((bf16[2048,1280]{1,0:T(8,128)(2,1)}), bf16[128,1280]{1,0:T(8,128)(2,1)}) %reduce-scatter.3.cloned.1.call-update) | async-done | bytes 327696 | tf_op jit(solution)/shard_map/reduce_scatter | solution.py:134
  464.6 1.7 slice_bitcast_fusion
  466.4 164.7 %all-gather.16.cloned.1.call-done = bf16[10240,1280]{1,0:T(8,128)(2,1)} async-done(((bf16[640,1280]{1,0:T(8,128)(2,1)}), bf16[10240,1280]{1,0:T(8,128)(2,1)}) %all-gather.16.cloned.1.call-update) | async-done | bytes 26214416 | tf_op jit(solution)/shard_map/all_gather | solution.py:148
  631.1 16.8 %reduce_sum.92 = bf16[640,1280]{1,0:T(8,128)(2,1)} reduce(bf16[16,640,1280]{2,1,0:T(8,128)(2,1)} %bitcast.86, bf16[]{:T(256)} %constant.23.clone.1), dimensions={0}, to_apply=%region_13.0 | reduce | flops 12288000 | bytes 27852802 | tf_op jit(solution)/shard_map/reduce_sum | solution.py:148
  (69 shorter events, 8.9 us)
Async XLA Ops:
  7.2 226.0 %copy-start = (bf16[1,128,5120]{2,1,0:T(8,128)(2,1)S(1)}, bf16[1,128,5120]{2,1,0:T(8,128)(2,1)}, u32[]{:S(2)}) copy-start(bf16[1,128,5120]{2,1,0:T(8,128)(2,1)} %param.9) | copy-start | bytes 3932164
  7.2 49.9 %copy-start.11 = (bf16[1,128,640]{2,1,0:T(8,128)(2,1)S(1)}, bf16[1,128,640]{2,1,0:T(8,128)(2,1)}, u32[]{:S(2)}) copy-start(bf16[1,128,640]{2,1,0:T(8,128)(2,1)} %param.6) | copy-start | bytes 491524
  7.2 57.3 %all-gather.12.cloned.1.call-start = ((), (), s32[]{:S(2)}) async-start(), calls=%async_computation.5 | async-start | bytes 2785280 | tf_op jit(solution)/shard_map/all_gather | solution.py:38
  7.9 109.6 %all-gather.14.cloned.1.call-start = ((), (), s32[]{:S(2)}) async-start(), calls=%async_computation.6 | async-start | bytes 2785280 | tf_op jit(solution)/shard_map/all_gather | solution.py:37
  8.7 224.5 %all-gather.10.cloned.1.call-start = ((), (), s32[]{:S(2)}) async-start(), calls=%async_computation.2 | async-start | bytes 8192000 | tf_op jit(solution)/shard_map/all_gather | solution.py:78
  9.4 369.6 %reduce-scatter.5.cloned.1.call-start = ((), (), s32[]{:S(2)}) async-start(), calls=%async_computation.4 | async-start | bytes 8192000 | tf_op jit(solution)/shard_map/reduce_scatter | solution.py:145
  57.3 63.4 %copy-start.7 = (bf16[2,64,5,128]{3,2,1,0:T(8,128)(2,1)}, bf16[2,64,5,128]{3,2,1,0:T(8,128)(2,1)S(1)}, u32[]{:S(2)}) copy-start(bf16[2,64,5,128]{3,2,1,0:T(8,128)(2,1)S(1)} %reshape_squeeze.6) | copy-start | bytes 491524
  120.7 117.4 %copy-start.2 = (bf16[2,256,5,128]{3,2,1,0:T(8,128)(2,1)}, bf16[2,256,5,128]{3,2,1,0:T(8,128)(2,1)S(1)}, u32[]{:S(2)}) copy-start(bf16[2,256,5,128]{3,2,1,0:T(8,128)(2,1)S(1)} %reshape.156) | copy-start | bytes 1966084
  241.1 0.7 copy-start.5
  246.3 0.7 copy-start.13
  246.4 218.3 %reduce-scatter.3.cloned.1.call-start = ((), (), s32[]{:S(2)}) async-start(), calls=%async_computation.3 | async-start | bytes 5570560 | tf_op jit(solution)/shard_map/reduce_scatter | solution.py:134
  247.3 0.7 copy-start.12
  250.7 2.0 copy-start.4
  250.7 3.0 copy-start.8
  253.0 0.7 copy-start.9
  277.8 101.2 %copy-start.6 = (bf16[2,64,5,128]{3,2,1,0:T(8,128)(2,1)S(1)}, bf16[2,64,5,128]{3,2,1,0:T(8,128)(2,1)}, u32[]{:S(2)}) copy-start(bf16[2,64,5,128]{3,2,1,0:T(8,128)(2,1)} %copy-done.5) | copy-start | bytes 491524
  277.8 102.2 %copy-start.3 = (bf16[2,256,5,128]{3,2,1,0:T(8,128)(2,1)S(1)}, bf16[2,256,5,128]{3,2,1,0:T(8,128)(2,1)}, u32[]{:S(2)}) copy-start(bf16[2,256,5,128]{3,2,1,0:T(8,128)(2,1)} %copy-done.2) | copy-start | bytes 1966084
  277.8 102.2 %copy-start.10 = (bf16[2,5,64,256]{3,2,1,0:T(8,128)(2,1)S(1)}, bf16[2,5,64,256]{3,2,1,0:T(8,128)(2,1)}, u32[]{:S(2)}) copy-start(bf16[2,5,64,256]{3,2,1,0:T(8,128)(2,1)} %copy-done.9) | copy-start | bytes 983044
  277.9 353.3 %all-gather.16.cloned.1.call-start = ((), (), s32[]{:S(2)}) async-start(), calls=%async_computation.7 | async-start | bytes 27852800 | tf_op jit(solution)/shard_map/all_gather | solution.py:148
  631.1 16.8 %copy-start.1 = (bf16[1,128,5120]{2,1,0:T(8,128)(2,1)S(1)}, bf16[1,128,5120]{2,1,0:T(8,128)(2,1)}, u32[]{:S(2)}) copy-start(bf16[1,128,5120]{2,1,0:T(8,128)(2,1)} %param.9) | copy-start | bytes 3932164
Sparse Core Ops, SparseCore 0:
  10.5 53.9 all-gather.11
  66.9 50.6 all-gather.13
  119.4 113.7 all-gather.9
  246.5 132.4 reduce-scatter.4
  382.5 82.0 reduce-scatter.2
  466.9 164.1 all-gather.15
